TPU v7x, 128 devices: a whole 4x4x4 slice. The times are simulated.
128 devices in a mesh: dp: 4 (over x), tensor: 32 (over y, z, core).
Axes of the slice: x: 4, y: 4, z: 4, core: 2. Of those that a mesh axis runs over, the one named last changes fastest.
Arguments:
- tokens: bfloat16 [16384, 2048], P(('dp', 'tensor')), may hold values from -6 to 6
- norm_gain: bfloat16 [2048], replicated, may hold values from 0.099609375 to 1.8984375
- routes: int32 [16384, 6], P(('dp', 'tensor')), may hold values from 0 to 31, all different within a row; in each aligned block of 128 rows (0 to 127, 128 to 255, ...) at most 32 rows name the same one
- route_gates: bfloat16 [16384, 6], P(('dp', 'tensor')), may hold values from 0.19921875 to 1
- lengths: int32 [24], replicated, may hold values from 1 to 1920, 16384 in all
- request_adapter: int32 [24], replicated, may hold values from 0 to 31
- adapter_slot: int32 [32], replicated, may hold values from 0 to 31, each once
- expert_gate: bfloat16 [32, 2048, 1408], P('tensor'), may hold values from -0.125 to 0.125
- expert_up: bfloat16 [32, 2048, 1408], P('tensor'), may hold values from -0.125 to 0.125
- expert_down: bfloat16 [32, 1408, 2048], P('tensor'), may hold values from -0.15625 to 0.15625
- shared_gate: bfloat16 [2048, 1408], P(None, 'dp'), may hold values from -0.125 to 0.125
- shared_up_weight: bfloat16 [2048, 1408], P(None, 'dp'), may hold values from -0.125 to 0.125
- shared_down: bfloat16 [1408, 2048], P('dp'), may hold values from -0.15625 to 0.15625
- adapter_down: bfloat16 [32, 2048, 16], P('dp'), may hold values from -0.125 to 0.125
- adapter_up: bfloat16 [32, 16, 2048], P('dp'), may hold values from -1.5 to 1.5
- head_weight: bfloat16 [2048, 65536], P(None, ('dp', 'tensor')), may hold values from -0.375 to 0.375
Outputs:
- sublayer_out: bfloat16 [16384, 2048], P(('dp', 'tensor'))
- last_norm: float32 [24], replicated
- block_logit: float32 [24, 32], P(None, 'tensor')
Inputs may be any that keep to these rules, and one draw needn't show every extreme that they name: `routes`: in each aligned block of 128 rows (the rows of one device), no expert is named by more than 32 rows, a bound that some block reaches. The lengths sum to 16384; the largest is exactly 1920. Each position of the store appears once: adapter a is stored at position adapter_slot[a] of adapter_down and adapter_up.
All inputs are finite; a program needn't handle non-finite values.
Results may differ from a plain program's by a relative error of at most 0.0066.
Values may be sent and summed in bfloat16 or wider, within the bound.
A program may use at most 128 MiB of HBM per device.

v0:
```python
import jax
import jax.numpy as jnp
from jax import lax
from jax.sharding import PartitionSpec as P

CAP = 32


def apply_norm(tokens, norm_gain):
    values = tokens.astype(jnp.float32)
    scaled = lax.rsqrt(jnp.mean(values * values, axis=-1, keepdims=True) + 1e-06)
    return (values * scaled * norm_gain.astype(jnp.float32)).astype(jnp.bfloat16)


def feed_forward(inputs, gate_mat, up_mat, down_mat):
    gate_portion = jnp.dot(inputs, gate_mat, preferred_element_type=jnp.float32)
    up_part = jnp.dot(inputs, up_mat, preferred_element_type=jnp.float32)
    hidden = (jax.nn.silu(gate_portion) * up_part).astype(jnp.bfloat16)
    return jnp.dot(hidden, down_mat, preferred_element_type=jnp.float32)


def token_slots(positions, lengths, request_adapter, adapter_slot):
    request_ends = jnp.cumsum(lengths)
    request = jnp.sum((request_ends[None, :] <= positions[:, None]).astype(jnp.int32), axis=1)
    request_pick = (
        request[:, None] == jnp.arange(request_adapter.shape[0], dtype=jnp.int32)[None, :]
    )
    adapter = jnp.sum(jnp.where(request_pick, request_adapter[None, :], 0), axis=1)
    adapter_pick = adapter[:, None] == jnp.arange(adapter_slot.shape[0], dtype=jnp.int32)[None, :]
    return jnp.sum(jnp.where(adapter_pick, adapter_slot[None, :], 0), axis=1)


def adapter_delta(inputs, slot_ids, down_store, up_store):
    held_count = down_store.shape[0]
    model_width = down_store.shape[1]
    rank_size = down_store.shape[2]
    flat_down = jnp.transpose(down_store, (1, 0, 2)).reshape(model_width, held_count * rank_size)
    low_rank = jnp.dot(inputs, flat_down, preferred_element_type=jnp.float32)
    low_rank = low_rank.reshape(inputs.shape[0], held_count, rank_size)
    keep_mask = slot_ids[:, None] == jnp.arange(held_count, dtype=jnp.int32)[None, :]
    low_rank = jnp.where(keep_mask[:, :, None], low_rank, 0.0).astype(jnp.bfloat16)
    low_rank = low_rank.reshape(inputs.shape[0], held_count * rank_size)
    flat_up = up_store.reshape(held_count * rank_size, up_store.shape[2])
    return jnp.dot(low_rank, flat_up, preferred_element_type=jnp.float32)


def local(
    tokens,
    norm_gain,
    routes,
    route_gates,
    lengths,
    request_adapter,
    adapter_slot,
    expert_gate,
    expert_up,
    expert_down,
    shared_gate,
    shared_up_weight,
    shared_down,
    adapter_down,
    adapter_up,
    head_weight,
):
    tok_rows = tokens.shape[0]
    model_width = tokens.shape[1]
    route_count = routes.shape[1]
    tensor_size = lax.axis_size("tensor")
    tensor_pos = lax.axis_index("tensor")
    data_pos = lax.axis_index("dp")
    local_experts = expert_gate.shape[0]
    all_experts = local_experts * tensor_size
    slot_range = jnp.arange(CAP, dtype=jnp.int32)
    normed = apply_norm(tokens, norm_gain)
    numbers = jnp.arange(all_experts, dtype=jnp.int32)
    route_hits = routes[:, :, None] == numbers[None, None, :]
    chosen = jnp.any(route_hits, axis=1)
    weight = jnp.sum(
        jnp.where(route_hits, route_gates[:, :, None], jnp.zeros((), jnp.bfloat16)), axis=1
    )
    slot_place = jnp.cumsum(chosen.astype(jnp.int32), axis=0) - 1
    pooled, pooled_routes = (
        lax.all_gather(normed, "tensor", axis=0, tiled=True),
        lax.all_gather(routes.astype(jnp.bfloat16), "tensor", axis=0, tiled=True),
    )
    pooled = pooled.reshape(tensor_size, tok_rows, model_width)
    source_routes = pooled_routes.astype(jnp.int32).reshape(tensor_size, tok_rows, route_count)
    own_numbers = tensor_pos * local_experts + jnp.arange(local_experts, dtype=jnp.int32)
    source_hits = source_routes[:, :, :, None] == own_numbers[None, None, None, :]
    source_chosen = jnp.any(source_hits, axis=2)
    source_place = jnp.cumsum(source_chosen.astype(jnp.int32), axis=1) - 1
    source_pick = source_chosen[:, :, :, None] & (
        source_place[:, :, :, None] == slot_range[None, None, None, :]
    )
    source_pick = jnp.where(source_pick, 1.0, 0.0).astype(jnp.bfloat16)
    incoming = jnp.einsum(
        "sijc,sid->sjcd", source_pick, pooled, preferred_element_type=jnp.float32
    ).astype(jnp.bfloat16)
    gate_portion = jnp.einsum(
        "secd,edf->secf", incoming, expert_gate, preferred_element_type=jnp.float32
    )
    up_part = jnp.einsum("secd,edf->secf", incoming, expert_up, preferred_element_type=jnp.float32)
    hidden = (jax.nn.silu(gate_portion) * up_part).astype(jnp.bfloat16)
    expert_out = jnp.einsum(
        "secf,efd->secd", hidden, expert_down, preferred_element_type=jnp.float32
    ).astype(jnp.bfloat16)
    returned_rows = lax.all_to_all(expert_out, "tensor", split_axis=0, concat_axis=0, tiled=True)
    returned_rows = returned_rows.reshape(all_experts, CAP, model_width)
    mixing_result = jnp.where(
        slot_place[:, :, None] == slot_range[None, None, :],
        weight[:, :, None],
        jnp.zeros((), jnp.bfloat16),
    )
    routed_output = jnp.einsum(
        "kbt,btw->kw", mixing_result, returned_rows, preferred_element_type=jnp.float32
    )
    own_base = (data_pos * tensor_size + tensor_pos) * tok_rows
    own_positions = own_base + jnp.arange(tok_rows, dtype=jnp.int32)
    peer_rows = lax.all_gather(normed, "dp", axis=0, tiled=True)
    shared_sum = lax.psum_scatter(
        feed_forward(peer_rows, shared_gate, shared_up_weight, shared_down),
        "dp",
        scatter_dimension=0,
        tiled=True,
    )
    own_slots = token_slots(own_positions, lengths, request_adapter, adapter_slot)
    store_down, store_up = (
        lax.all_gather(adapter_down, "dp", axis=0, tiled=True),
        lax.all_gather(adapter_up, "dp", axis=0, tiled=True),
    )
    summed = routed_output + shared_sum + adapter_delta(normed, own_slots, store_down, store_up)
    sublayer_out = summed.astype(jnp.bfloat16)
    request_ends = jnp.cumsum(lengths)
    last_pick = jnp.where(request_ends[:, None] - 1 == own_positions[None, :], 1.0, 0.0).astype(
        jnp.bfloat16
    )
    last_part = jnp.dot(last_pick, sublayer_out, preferred_element_type=jnp.float32)
    last_states = lax.psum(last_part, ("dp", "tensor"))
    last_norm = jnp.sqrt(jnp.sum(last_states * last_states, axis=1))
    logits = jnp.dot(
        last_states.astype(jnp.bfloat16), head_weight, preferred_element_type=jnp.float32
    )
    block_logit = lax.pmax(jnp.max(logits, axis=1), "dp")
    return (sublayer_out, last_norm, block_logit[:, None])


def solution(mesh):
    placed = (
        P(("dp", "tensor"), None),
        P(),
        P(("dp", "tensor"), None),
        P(("dp", "tensor"), None),
        P(),
        P(),
        P(),
        P("tensor", None, None),
        P("tensor", None, None),
        P("tensor", None, None),
        P(None, "dp"),
        P(None, "dp"),
        P("dp", None),
        P("dp", None, None),
        P("dp", None, None),
        P(None, ("dp", "tensor")),
    )
    return jax.shard_map(
        local,
        mesh=mesh,
        in_specs=placed,
        out_specs=(P(("dp", "tensor"), None), P(), P(None, "tensor")),
        check_vma=False,
    )
```

profile of v0, /device:TPU:0, one launch (start us, length us, event | category | flops | bytes accessed | tf_op | source)
XLA Modules:
  0.0 401.9 jit_solution(9235097486257809376)
XLA Ops:
  7.2 0.0 all-gather.7.cloned.1.call-start
  7.2 0.9 convert_element_type.84
  8.1 1.3 fusion.41
  9.4 2.0 fusion.43
  11.4 0.0 all-gather.7.cloned.1.call-update
  11.5 0.0 all-gather.5.cloned.1.call-start
  11.5 0.7 all-gather.5.cloned.1.call-update
  12.2 0.0 reduce-scatter.2.cloned.1.call-start
  12.3 32.6 %all-gather.7.cloned.1.call-done = bf16[512,2048]{1,0:T(8,128)(2,1)} async-done(((bf16[128,2048]{1,0:T(8,128)(2,1)}), bf16[512,2048]{1,0:T(8,128)(2,1)}) %all-gather.7.cloned.1.call-update) | async-done | bytes 2097168 | tf_op jit(solution)/shard_map/all_gather | solution.py:119
  44.9 3.8 fusion.82
  48.7 6.3 %fusion.32 = f32[512,2048]{1,0:T(8,128)} fusion(bf16[352,2048]{1,0:T(8,128)(2,1)S(1)} %copy-done.8, bf16[512,2048]{1,0:T(8,128)(2,1)} %all-gather.7.cloned.1.call-done, bf16[2048,352]{0,1:T(8,128)(2,1)} %param.27, f32[512,352]{0,1:T(8,128)} %fusion.82), kind=kOutput, calls=%fused_computation.29 | convolution fusion | flops 1477476352 | bytes 9895936 | tf_op jit(solution)/shard_map/dot_general | solution.py:19
  55.0 0.0 reduce-scatter.2.cloned.1.call-update
  55.0 0.0 all-gather.11.cloned.1.call-start
  55.1 1.0 copy-done.4
  56.0 1.1 copy.47
  57.2 24.6 %all_gather.15 = bf16[4096,6]{0,1:T(8,128)(2,1)S(1)} all-gather(bf16[128,6]{0,1:T(8,128)(2,1)S(1)} %convert_element_type.79), channel_id=1, replica_groups=mesh['dp'=4,'tensor'=32] {'tensor'}, dimensions={0}, use_global_device_ids=true | all-gather | bytes 50688 | tf_op jit(solution)/shard_map/all_gather | solution.py:84
  81.7 0.1 fusion.63
  81.8 0.3 reduce_window_sum.31
  82.1 38.3 %all-gather.5.cloned.1.call-done = bf16[4096,2048]{1,0:T(8,128)(2,1)} async-done(((bf16[128,2048]{1,0:T(8,128)(2,1)}), bf16[4096,2048]{1,0:T(8,128)(2,1)}) %all-gather.5.cloned.1.call-update) | async-done | bytes 16777232 | tf_op jit(solution)/shard_map/all_gather | solution.py:83
  120.4 8.1 %convolution_convert_fusion = bf16[32,32,2048]{2,1,0:T(8,128)(2,1)S(1)} fusion(bf16[32,128,2048]{2,1,0:T(8,128)(2,1)} %bitcast.109, s32[32,128]{1,0:T(8,128)S(1)} %broadcast_add_fusion.1, pred[32,128]{1,0:T(8,128)(4,1)S(1)} %bitcast.111), kind=kOutput, calls=%fused_computation.16 | convolution fusion | flops 539492352 | bytes 20992000 | tf_op jit(solution)/shard_map/sijc,sid->sjcd/dot_general | solution.py:96
  128.5 2.1 copy-done.1
  130.6 10.7 %fusion.3 = f32[32,32,1408]{2,1,0:T(8,128)} fusion(bf16[32,32,2048]{2,1,0:T(8,128)(2,1)S(1)} %convolution_convert_fusion, bf16[1,2048,1408]{2,1,0:T(8,128)(2,1)} %param.24), kind=kOutput, calls=%fused_computation.4 | convolution fusion | flops 5905580032 | bytes 15728640 | tf_op jit(solution)/shard_map/secd,edf->secf/dot_general | solution.py:102
  141.3 21.0 %convert_bitcast_fusion = bf16[32,1,32,2048]{3,2,1,0:T(8,128)(2,1)} fusion(bf16[1,1408,2048]{2,1,0:T(8,128)(2,1)} %param.25, f32[32,32,1408]{2,1,0:T(8,128)} %fusion.3, bf16[32,32,2048]{2,1,0:T(8,128)(2,1)} %copy-done.1, bf16[1,2048,1408]{2,1,0:T(8,128)(2,1)} %param.23), kind=kOutput, calls=%fused_computation.15 | convolution fusion | flops 11821907968 | bytes 25690112 | tf_op jit(solution)/shard_map/secf,efd->secd/dot_general | solution.py:104
  162.4 5.2 %all-to-all-start = ((bf16[32,1,32,2048]{3,2,1,0:T(8,128)(2,1)}), bf16[32,1,32,2048]{3,2,1,0:T(8,128)(2,1)}, u32[]{:S(2)}, u32[]{:S(2)}) async-start(bf16[32,1,32,2048]{3,2,1,0:T(8,128)(2,1)} %convert_bitcast_fusion), calls=%async_computation | async-start | bytes 8388608 | tf_op jit(solution)/shard_map/all_to_all | solution.py:107
  167.6 0.0 all-gather.9.cloned.1.call-start
  167.7 0.5 all-gather.9.cloned.1.call-update
  168.2 0.3 all-reduce.2.cloned.1.call-start
  168.5 0.1 copy.42
  168.6 0.2 reduce_window_sum.30
  168.8 0.1 copy.43
  168.8 0.1 copy.45
  168.9 0.1 reduce-window.7
  169.0 0.1 reduce.2
  169.1 0.1 convert_reduce_fusion
  169.2 0.1 select_reduce_fusion.1
  169.3 0.1 select_reduce_fusion
  169.5 0.0 reduce-scatter.2.cloned.1.call-done
  169.5 50.9 %all-to-all-done = bf16[32,1,32,2048]{3,2,1,0:T(8,128)(2,1)} async-done(((bf16[32,1,32,2048]{3,2,1,0:T(8,128)(2,1)}), bf16[32,1,32,2048]{3,2,1,0:T(8,128)(2,1)}, u32[]{:S(2)}, u32[]{:S(2)}) %all-to-all-start) | async-done | bytes 4194336 | tf_op jit(solution)/shard_map/all_to_all | solution.py:107
  220.4 4.3 %fusion.23 = f32[128,2048]{1,0:T(8,128)} fusion(f32[128,2048]{1,0:T(8,128)} %reduce-scatter.2.cloned.1.call-done, bf16[32,1,32,2048]{3,2,1,0:T(8,128)(2,1)} %all-to-all-done, s32[128,32]{0,1:T(8,128)S(1)} %copy.43, bf16[128,32]{0,1:T(8,128)(2,1)S(1)} %fusion.68), kind=kOutput, calls=%fused_computation.21 | convolution fusion | flops 537395200 | bytes 6316032 | tf_op jit(solution)/shard_map/kbt,btw->kw/dot_general | solution.py:114
  224.7 9.1 %all-gather.9.cloned.1.call-done = bf16[32,2048,16]{1,2,0:T(8,128)(2,1)} async-done(((bf16[8,2048,16]{1,2,0:T(8,128)(2,1)}), bf16[32,2048,16]{1,2,0:T(8,128)(2,1)}) %all-gather.9.cloned.1.call-update) | async-done | bytes 2097168 | tf_op jit(solution)/shard_map/all_gather | solution.py:128
  233.7 4.5 %fusion.26 = bf16[128,2048]{1,0:T(8,128)(2,1)S(1)} fusion(f32[128,2048]{1,0:T(8,128)} %fusion.23, bf16[32,16,2048]{2,0,1:T(8,128)(2,1)} %all-gather.11.cloned.1.call-done, bf16[32,16,2048]{2,1,0:T(8,128)(2,1)} %bitcast.110, bf16[128,2048]{1,0:T(8,128)(2,1)S(1)} %copy-done.2, pred[128,32]{0,1:T(8,128)(4,1)S(1)} %iota_compare_fusion.3), kind=kOutput, calls=%fused_computation.22 | convolution fusion | flops 537526272 | bytes 6295552 | tf_op jit(solution)/shard_map/dot_general | solution.py:44
  238.3 0.9 fusion.69
  239.2 0.0 all-reduce.2.cloned.1.call-update
  239.2 143.1 %all-reduce.2.cloned.1.call-done = f32[24,2048]{1,0:T(8,128)} async-done(((f32[24,2048]{1,0:T(8,128)}), f32[24,2048]{1,0:T(8,128)}) %all-reduce.2.cloned.1.call-update) | async-done | bytes 196624 | tf_op jit(solution)/shard_map/psum | solution.py:138
  382.3 1.4 convolution_reduce_fusion
  383.7 9.7 %pmax.7 = f32[24,1]{0,1:T(1,128)} all-reduce(f32[24,1]{0,1:T(1,128)S(1)} %bitcast.112), channel_id=1, replica_groups=mesh['dp'=4,'tensor'=32] {'dp'}, use_global_device_ids=true, to_apply=%region_14.15 | all-reduce | flops 24 | bytes 192 | tf_op jit(solution)/shard_map/pmax | solution.py:143
  393.5 1.1 multiply_reduce_fusion
  394.6 0.5 sqrt.3
  (33 shorter events, 0.2 us)
Async XLA Ops:
  7.2 375.2 %copy-start = (bf16[2048,512]{1,0:T(8,128)(2,1)S(1)}, bf16[2048,512]{1,0:T(8,128)(2,1)}, u32[]{:S(2)}) copy-start(bf16[2048,512]{1,0:T(8,128)(2,1)} %param.31) | copy-start | bytes 6291460
  7.2 41.5 %copy-start.8 = (bf16[352,2048]{1,0:T(8,128)(2,1)S(1)}, bf16[352,2048]{1,0:T(8,128)(2,1)}, u32[]{:S(2)}) copy-start(bf16[352,2048]{1,0:T(8,128)(2,1)} %param.28) | copy-start | bytes 4325380
  7.2 37.7 %all-gather.7.cloned.1.call-start = ((), (), s32[]{:S(2)}) async-start(), calls=%async_computation.3 | async-start | bytes 2621440 | tf_op jit(solution)/shard_map/all_gather | solution.py:119
  11.5 109.0 %all-gather.5.cloned.1.call-start = ((), (), s32[]{:S(2)}) async-start(), calls=%async_computation.2 | async-start | bytes 17301504 | tf_op jit(solution)/shard_map/all_gather | solution.py:83
  12.2 157.3 %reduce-scatter.2.cloned.1.call-start = ((), (), s32[]{:S(2)}) async-start(), calls=%async_computation.4 | async-start | bytes 5242880 | tf_op jit(solution)/shard_map/reduce_scatter | solution.py:120
  55.0 1.0 copy-start.4
  55.0 2.1 copy-start.5
  55.0 169.6 %all-gather.11.cloned.1.call-start = ((), (), s32[]{:S(2)}) async-start(), calls=%async_computation.6 | async-start | bytes 2621440 | tf_op jit(solution)/shard_map/all_gather | solution.py:129
  128.5 2.1 copy-start.1
  162.3 6.5 %copy-start.7 = (s32[24]{0:T(128)S(1)}, s32[24]{0:T(128)}, u32[]{:S(2)}) copy-start(s32[24]{0:T(128)} %param.20) | copy-start | bytes 292
  162.3 6.9 %copy-start.9 = (s32[24]{0:T(128)S(1)}, s32[24]{0:T(128)}, u32[]{:S(2)}) copy-start(s32[24]{0:T(128)} %param.21) | copy-start | bytes 292
  162.3 7.0 %copy-start.10 = (s32[32]{0:T(128)S(1)}, s32[32]{0:T(128)}, u32[]{:S(2)}) copy-start(s32[32]{0:T(128)} %param.22) | copy-start | bytes 388
  162.4 7.1 %copy-start.6 = (bf16[128,6]{0,1:T(8,128)(2,1)S(1)}, bf16[128,6]{0,1:T(8,128)(2,1)}, u32[]{:S(2)}) copy-start(bf16[128,6]{0,1:T(8,128)(2,1)} %param.19) | copy-start | bytes 4612
  162.4 58.0 %all-to-all-start = ((bf16[32,1,32,2048]{3,2,1,0:T(8,128)(2,1)}), bf16[32,1,32,2048]{3,2,1,0:T(8,128)(2,1)}, u32[]{:S(2)}, u32[]{:S(2)}) async-start(bf16[32,1,32,2048]{3,2,1,0:T(8,128)(2,1)} %convert_bitcast_fusion), calls=%async_computation | async-start | bytes 8388608 | tf_op jit(solution)/shard_map/all_to_all | solution.py:107
  167.6 66.1 %copy-start.2 = (bf16[128,2048]{1,0:T(8,128)(2,1)S(1)}, bf16[128,2048]{1,0:T(8,128)(2,1)}, u32[]{:S(2)}) copy-start(bf16[128,2048]{1,0:T(8,128)(2,1)} %fusion.43) | copy-start | bytes 1572868
  167.6 66.1 %all-gather.9.cloned.1.call-start = ((), (), s32[]{:S(2)}) async-start(), calls=%async_computation.5 | async-start | bytes 2621440 | tf_op jit(solution)/shard_map/all_gather | solution.py:128
  168.2 214.1 %all-reduce.2.cloned.1.call-start = ((), (), s32[]{:S(2)}) async-start(), calls=%async_computation.7 | async-start | bytes 393216 | tf_op jit(solution)/shard_map/psum | solution.py:138
  238.3 156.8 %copy-start.3 = (bf16[128,2048]{1,0:T(8,128)(2,1)}, bf16[128,2048]{1,0:T(8,128)(2,1)S(1)}, u32[]{:S(2)}) copy-start(bf16[128,2048]{1,0:T(8,128)(2,1)S(1)} %fusion.26) | copy-start | bytes 1572868
Sparse Core Ops, SparseCore 0:
  11.6 33.2 all-gather.6
  47.7 72.6 all-gather.4
  122.8 46.1 reduce-scatter.1
  170.7 30.5 all-gather.10
  202.9 30.8 all-gather.8
  239.3 142.9 all-reduce.1
where the time goes:
time: 402 us
  waiting for transfers between devices  275 us (68%)
  matrix products  61.1 us (15%)
  blocking collectives  34.3 us (9%)
  between operations  14.3 us (4%)
  other arithmetic  6.28 us (2%)
  starting transfers between devices  5.69 us (1%)
  local copies, waits for them, and re-layouts  4.94 us (1%)
    psum x1, waiting for transfers between devices, local(): last_states = lax.psum(last_part, ('dp', 'tensor'))  143 us
    all_to_all x1, waiting for transfers between devices, local(): lax.all_to_all(expert_out, 'tensor', split_axis=0, concat_axis=0, tiled=T...  50.9 us
    all_gather x1, waiting for transfers between devices, local(): lax.all_gather(normed, 'tensor', axis=0, tiled=True)  38.3 us
    all_gather x1, waiting for transfers between devices, local(): peer_rows = lax.all_gather(normed, 'dp', axis=0, tiled=True)  32.6 us
    all_gather x1, blocking collectives, local(): lax.all_gather(routes.astype(jnp.bfloat16), 'tensor', axis=0, tiled=True)  24.6 us
    dot_general x1, matrix products, local(): jnp.einsum('secf,efd->secd', hidden, expert_down, preferred_element_type=...  21 us
    dot_general x1, matrix products, local(): jnp.einsum('secd,edf->secf', incoming, expert_up, preferred_element_type=...  10.7 us
    pmax x1, blocking collectives, local(): block_logit = lax.pmax(jnp.max(logits, axis=1), 'dp')  9.75 us
  transfers between devices with their start and end apart: 7, of which 5 were waited for; matrix products, arithmetic and copies ran while one was open for 14% of the time, Pallas kernels for 0%

commit v1 on v0

--- a/solution.py
+++ b/solution.py
@@ -135,7 +135,7 @@
         jnp.bfloat16
     )
     last_part = jnp.dot(last_pick, sublayer_out, preferred_element_type=jnp.float32)
-    last_states = lax.psum(last_part, ("dp", "tensor"))
+    last_states = jnp.sum(lax.all_gather(last_part, ("dp", "tensor")), axis=0)
     last_norm = jnp.sqrt(jnp.sum(last_states * last_states, axis=1))
     logits = jnp.dot(
         last_states.astype(jnp.bfloat16), head_weight, preferred_element_type=jnp.float32

time: 402 us -> 361 us (0.90)
  waiting for transfers between devices: 275 us -> 227 us
  other arithmetic: 6.28 us -> 14.5 us
    psum x1 -> x0, waiting for transfers between devices: 143 us -> none  [local(): last_states = lax.psum(last_part, ('dp', 'tensor'))]
    all_gather x0 -> x1, waiting for transfers between devices: none -> 93.3 us  [local(): last_states = jnp.sum(lax.all_gather(last_part, ('dp', 'tensor')), axis=0)]
    reduce_sum x0 -> x1, other arithmetic: none -> 9.17 us  [local(): last_states = jnp.sum(lax.all_gather(last_part, ('dp', 'tensor')), axis=0)]
    all_gather x1, waiting for transfers between devices: 0.01 us -> 9.13 us  [local(): lax.all_gather(adapter_up, 'dp', axis=0, tiled=True)]
    all_gather x1, waiting for transfers between devices: 9.08 us -> 0.01 us  [local(): lax.all_gather(adapter_down, 'dp', axis=0, tiled=True)]
  transfers between devices with their start and end apart: 7 -> 7, of which waited for: 5 -> 5; matrix products, arithmetic and copies ran while one was open for 14% -> 16% of each run, Pallas kernels for 0% -> 0%
where the time goes in v1:
time: 361 us
  waiting for transfers between devices  227 us (63%)
  matrix products  60.2 us (17%)
  blocking collectives  35.4 us (10%)
  other arithmetic  14.5 us (4%)
  between operations  14.3 us (4%)
  starting transfers between devices  5.65 us (2%)
  local copies, waits for them, and re-layouts  4.07 us (1%)
    all_gather x1, waiting for transfers between devices, local(): last_states = jnp.sum(lax.all_gather(last_part, ('dp', 'tensor')), axis=0)  93.3 us
    all_to_all x1, waiting for transfers between devices, local(): lax.all_to_all(expert_out, 'tensor', split_axis=0, concat_axis=0, tiled=T...  50.3 us
    all_gather x1, waiting for transfers between devices, local(): lax.all_gather(normed, 'tensor', axis=0, tiled=True)  40 us
    all_gather x1, waiting for transfers between devices, local(): peer_rows = lax.all_gather(normed, 'dp', axis=0, tiled=True)  32.6 us
    all_gather x1, blocking collectives, local(): lax.all_gather(routes.astype(jnp.bfloat16), 'tensor', axis=0, tiled=True)  24.5 us
    dot_general x1, matrix products, local(): jnp.einsum('secf,efd->secd', hidden, expert_down, preferred_element_type=...  21 us
    pmax x1, blocking collectives, local(): block_logit = lax.pmax(jnp.max(logits, axis=1), 'dp')  10.9 us
    dot_general x1, matrix products, local(): jnp.einsum('secd,edf->secf', incoming, expert_up, preferred_element_type=...  10.8 us
  transfers between devices with their start and end apart: 7, of which 5 were waited for; matrix products, arithmetic and copies ran while one was open for 16% of the time, Pallas kernels for 0%

profile of v1, /device:TPU:0, one launch (start us, length us, event | category | flops | bytes accessed | tf_op | source)
XLA Modules:
  0.0 360.7 jit_solution(14780994323421316763)
XLA Ops:
  7.2 0.0 all-gather.9.cloned.1.call-start
  7.2 1.4 fusion.41
  8.7 0.7 convert_element_type.84
  9.3 2.0 fusion.43
  11.4 0.0 all-gather.9.cloned.1.call-update
  11.4 0.0 all-gather.7.cloned.1.call-start
  11.4 0.7 all-gather.7.cloned.1.call-update
  12.1 0.0 reduce-scatter.2.cloned.1.call-start
  12.2 32.6 %all-gather.9.cloned.1.call-done = bf16[512,2048]{1,0:T(8,128)(2,1)} async-done(((bf16[128,2048]{1,0:T(8,128)(2,1)}), bf16[512,2048]{1,0:T(8,128)(2,1)}) %all-gather.9.cloned.1.call-update) | async-done | bytes 2097168 | tf_op jit(solution)/shard_map/all_gather | solution.py:119
  44.8 3.8 %fusion.82 = f32[512,352]{0,1:T(8,128)} fusion(bf16[512,2048]{1,0:T(8,128)(2,1)} %all-gather.9.cloned.1.call-done, bf16[2048,352]{0,1:T(8,128)(2,1)} %param.26), kind=kOutput, calls=%fused_computation.91 | convolution fusion | flops 738197504 | bytes 4259840 | tf_op jit(solution)/shard_map/dot_general | solution.py:16
  48.6 6.3 %fusion.32 = f32[512,2048]{1,0:T(8,128)} fusion(bf16[352,2048]{1,0:T(8,128)(2,1)S(1)} %copy-done.8, bf16[512,2048]{1,0:T(8,128)(2,1)} %all-gather.9.cloned.1.call-done, bf16[2048,352]{0,1:T(8,128)(2,1)} %param.27, f32[512,352]{0,1:T(8,128)} %fusion.82), kind=kOutput, calls=%fused_computation.29 | convolution fusion | flops 1477476352 | bytes 9895936 | tf_op jit(solution)/shard_map/dot_general | solution.py:19
  54.9 0.0 reduce-scatter.2.cloned.1.call-update
  55.0 0.0 all-gather.11.cloned.1.call-start
  55.0 0.5 all-gather.11.cloned.1.call-update
  55.5 0.1 copy-done.5
  55.6 24.5 %all_gather.21 = bf16[4096,6]{0,1:T(8,128)(2,1)S(1)} all-gather(bf16[128,6]{0,1:T(8,128)(2,1)S(1)} %convert_element_type.79), channel_id=1, replica_groups=mesh['dp'=4,'tensor'=32] {'tensor'}, dimensions={0}, use_global_device_ids=true | all-gather | bytes 50688 | tf_op jit(solution)/shard_map/all_gather | solution.py:84
  80.2 0.1 fusion.63
  80.2 0.3 reduce_window_sum.31
  80.5 40.0 %all-gather.7.cloned.1.call-done = bf16[4096,2048]{1,0:T(8,128)(2,1)} async-done(((bf16[128,2048]{1,0:T(8,128)(2,1)}), bf16[4096,2048]{1,0:T(8,128)(2,1)}) %all-gather.7.cloned.1.call-update) | async-done | bytes 16777232 | tf_op jit(solution)/shard_map/all_gather | solution.py:83
  120.5 8.1 %convolution_convert_fusion = bf16[32,32,2048]{2,1,0:T(8,128)(2,1)S(1)} fusion(bf16[32,128,2048]{2,1,0:T(8,128)(2,1)} %bitcast.110, s32[32,128]{1,0:T(8,128)S(1)} %broadcast_add_fusion.1, pred[32,128]{1,0:T(8,128)(4,1)S(1)} %bitcast.113), kind=kOutput, calls=%fused_computation.16 | convolution fusion | flops 539492352 | bytes 20992000 | tf_op jit(solution)/shard_map/sijc,sid->sjcd/dot_general | solution.py:96
  128.6 2.1 copy-done.1
  130.7 10.8 %fusion.3 = f32[32,32,1408]{2,1,0:T(8,128)} fusion(bf16[32,32,2048]{2,1,0:T(8,128)(2,1)S(1)} %convolution_convert_fusion, bf16[1,2048,1408]{2,1,0:T(8,128)(2,1)} %param.24), kind=kOutput, calls=%fused_computation.4 | convolution fusion | flops 5905580032 | bytes 15728640 | tf_op jit(solution)/shard_map/secd,edf->secf/dot_general | solution.py:102
  141.4 21.0 %convert_bitcast_fusion = bf16[32,1,32,2048]{3,2,1,0:T(8,128)(2,1)} fusion(bf16[1,1408,2048]{2,1,0:T(8,128)(2,1)} %param.25, f32[32,32,1408]{2,1,0:T(8,128)} %fusion.3, bf16[32,32,2048]{2,1,0:T(8,128)(2,1)} %copy-done.1, bf16[1,2048,1408]{2,1,0:T(8,128)(2,1)} %param.23), kind=kOutput, calls=%fused_computation.15 | convolution fusion | flops 11821907968 | bytes 25690112 | tf_op jit(solution)/shard_map/secf,efd->secd/dot_general | solution.py:104
  162.5 5.2 %all-to-all-start = ((bf16[32,1,32,2048]{3,2,1,0:T(8,128)(2,1)}), bf16[32,1,32,2048]{3,2,1,0:T(8,128)(2,1)}, u32[]{:S(2)}, u32[]{:S(2)}) async-start(bf16[32,1,32,2048]{3,2,1,0:T(8,128)(2,1)} %convert_bitcast_fusion), calls=%async_computation | async-start | bytes 8388608 | tf_op jit(solution)/shard_map/all_to_all | solution.py:107
  167.7 0.0 all-gather.13.cloned.1.call-start
  167.7 1.1 copy.47
  168.9 0.3 all-gather.15.cloned.1.call-start
  169.2 0.1 copy.45
  169.3 0.1 reduce.2
  169.4 0.1 copy.42
  169.5 0.2 reduce_window_sum.30
  169.7 0.1 copy.43
  169.8 0.1 convert_reduce_fusion
  169.9 0.1 select_reduce_fusion.1
  170.0 0.1 select_reduce_fusion
  170.1 0.0 reduce-scatter.2.cloned.1.call-done
  170.2 50.3 %all-to-all-done = bf16[32,1,32,2048]{3,2,1,0:T(8,128)(2,1)} async-done(((bf16[32,1,32,2048]{3,2,1,0:T(8,128)(2,1)}), bf16[32,1,32,2048]{3,2,1,0:T(8,128)(2,1)}, u32[]{:S(2)}, u32[]{:S(2)}) %all-to-all-start) | async-done | bytes 4194336 | tf_op jit(solution)/shard_map/all_to_all | solution.py:107
  220.5 4.3 %fusion.23 = f32[128,2048]{1,0:T(8,128)} fusion(f32[128,2048]{1,0:T(8,128)} %reduce-scatter.2.cloned.1.call-done, bf16[32,1,32,2048]{3,2,1,0:T(8,128)(2,1)} %all-to-all-done, s32[128,32]{0,1:T(8,128)S(1)} %copy.43, bf16[128,32]{0,1:T(8,128)(2,1)S(1)} %fusion.68), kind=kOutput, calls=%fused_computation.21 | convolution fusion | flops 537395200 | bytes 6316032 | tf_op jit(solution)/shard_map/kbt,btw->kw/dot_general | solution.py:114
  224.7 9.1 %all-gather.13.cloned.1.call-done = bf16[32,16,2048]{2,0,1:T(8,128)(2,1)} async-done(((bf16[8,16,2048]{2,0,1:T(8,128)(2,1)}), bf16[32,16,2048]{2,0,1:T(8,128)(2,1)}) %all-gather.13.cloned.1.call-update) | async-done | bytes 2097168 | tf_op jit(solution)/shard_map/all_gather | solution.py:129
  233.9 4.5 %fusion.26 = bf16[128,2048]{1,0:T(8,128)(2,1)S(1)} fusion(f32[128,2048]{1,0:T(8,128)} %fusion.23, bf16[32,16,2048]{2,0,1:T(8,128)(2,1)} %all-gather.13.cloned.1.call-done, bf16[32,16,2048]{2,1,0:T(8,128)(2,1)} %bitcast.112, bf16[128,2048]{1,0:T(8,128)(2,1)S(1)} %copy-done.2, pred[128,32]{0,1:T(8,128)(4,1)S(1)} %iota_compare_fusion.3), kind=kOutput, calls=%fused_computation.22 | convolution fusion | flops 537526272 | bytes 6295552 | tf_op jit(solution)/shard_map/dot_general | solution.py:44
  238.4 0.9 fusion.69
  239.3 0.0 all-gather.15.cloned.1.call-update
  239.3 93.3 %all-gather.15.cloned.1.call-done = f32[3072,2048]{1,0:T(8,128)} async-done(((f32[24,2048]{1,0:T(8,128)}), f32[3072,2048]{1,0:T(8,128)}) %all-gather.15.cloned.1.call-update) | async-done | bytes 25165840 | tf_op jit(solution)/shard_map/all_gather | solution.py:138
  332.6 9.2 %reduce_sum.71 = f32[24,2048]{1,0:T(8,128)S(1)} reduce(f32[128,24,2048]{2,1,0:T(8,128)} %bitcast.111, f32[]{:T(128)} %constant.44.clone.1), dimensions={0}, to_apply=%region_11.12 | reduce | flops 6242304 | bytes 25362436 | tf_op jit(solution)/shard_map/reduce_sum | solution.py:138
  341.8 0.1 multiply_reduce_fusion
  341.9 0.5 convolution_reduce_fusion
  342.4 0.5 sqrt.3
  342.9 10.9 %pmax.7 = f32[24,1]{0,1:T(1,128)} all-reduce(f32[24,1]{0,1:T(1,128)S(1)} %bitcast.114), channel_id=1, replica_groups=mesh['dp'=4,'tensor'=32] {'dp'}, use_global_device_ids=true, to_apply=%region_14.15 | all-reduce | flops 24 | bytes 192 | tf_op jit(solution)/shard_map/pmax | solution.py:143
  (34 shorter events, 0.2 us)
Async XLA Ops:
  7.2 334.7 %copy-start = (bf16[2048,512]{1,0:T(8,128)(2,1)S(1)}, bf16[2048,512]{1,0:T(8,128)(2,1)}, u32[]{:S(2)}) copy-start(bf16[2048,512]{1,0:T(8,128)(2,1)} %param.31) | copy-start | bytes 6291460
  7.2 41.4 %copy-start.8 = (bf16[352,2048]{1,0:T(8,128)(2,1)S(1)}, bf16[352,2048]{1,0:T(8,128)(2,1)}, u32[]{:S(2)}) copy-start(bf16[352,2048]{1,0:T(8,128)(2,1)} %param.28) | copy-start | bytes 4325380
  7.2 37.6 %all-gather.9.cloned.1.call-start = ((), (), s32[]{:S(2)}) async-start(), calls=%async_computation.3 | async-start | bytes 2621440 | tf_op jit(solution)/shard_map/all_gather | solution.py:119
  11.4 109.1 %all-gather.7.cloned.1.call-start = ((), (), s32[]{:S(2)}) async-start(), calls=%async_computation.2 | async-start | bytes 17301504 | tf_op jit(solution)/shard_map/all_gather | solution.py:83
  12.1 158.0 %reduce-scatter.2.cloned.1.call-start = ((), (), s32[]{:S(2)}) async-start(), calls=%async_computation.4 | async-start | bytes 5242880 | tf_op jit(solution)/shard_map/reduce_scatter | solution.py:120
  54.9 0.7 copy-start.5
  55.0 169.8 %all-gather.11.cloned.1.call-start = ((), (), s32[]{:S(2)}) async-start(), calls=%async_computation.5 | async-start | bytes 2621440 | tf_op jit(solution)/shard_map/all_gather | solution.py:128
  128.6 2.1 copy-start.1
  162.4 5.3 %copy-start.4 = (bf16[8,16,2048]{2,1,0:T(8,128)(2,1)S(1)}, bf16[8,16,2048]{2,1,0:T(8,128)(2,1)}, u32[]{:S(2)}) copy-start(bf16[8,16,2048]{2,1,0:T(8,128)(2,1)} %param.30) | copy-start | bytes 1572868
  162.4 6.7 %copy-start.7 = (s32[24]{0:T(128)S(1)}, s32[24]{0:T(128)}, u32[]{:S(2)}) copy-start(s32[24]{0:T(128)} %param.20) | copy-start | bytes 292
  162.4 7.4 %copy-start.9 = (s32[24]{0:T(128)S(1)}, s32[24]{0:T(128)}, u32[]{:S(2)}) copy-start(s32[24]{0:T(128)} %param.21) | copy-start | bytes 292
  162.5 7.5 %copy-start.10 = (s32[32]{0:T(128)S(1)}, s32[32]{0:T(128)}, u32[]{:S(2)}) copy-start(s32[32]{0:T(128)} %param.22) | copy-start | bytes 388
  162.5 7.6 %copy-start.6 = (bf16[128,6]{0,1:T(8,128)(2,1)S(1)}, bf16[128,6]{0,1:T(8,128)(2,1)}, u32[]{:S(2)}) copy-start(bf16[128,6]{0,1:T(8,128)(2,1)} %param.19) | copy-start | bytes 4612
  162.5 58.0 %all-to-all-start = ((bf16[32,1,32,2048]{3,2,1,0:T(8,128)(2,1)}), bf16[32,1,32,2048]{3,2,1,0:T(8,128)(2,1)}, u32[]{:S(2)}, u32[]{:S(2)}) async-start(bf16[32,1,32,2048]{3,2,1,0:T(8,128)(2,1)} %convert_bitcast_fusion), calls=%async_computation | async-start | bytes 8388608 | tf_op jit(solution)/shard_map/all_to_all | solution.py:107
  167.7 66.2 %copy-start.2 = (bf16[128,2048]{1,0:T(8,128)(2,1)S(1)}, bf16[128,2048]{1,0:T(8,128)(2,1)}, u32[]{:S(2)}) copy-start(bf16[128,2048]{1,0:T(8,128)(2,1)} %fusion.43) | copy-start | bytes 1572868
  167.7 66.2 %all-gather.13.cloned.1.call-start = ((), (), s32[]{:S(2)}) async-start(), calls=%async_computation.6 | async-start | bytes 2621440 | tf_op jit(solution)/shard_map/all_gather | solution.py:129
  168.9 163.7 %all-gather.15.cloned.1.call-start = ((), (), s32[]{:S(2)}) async-start(), calls=%async_computation.7 | async-start | bytes 25362432 | tf_op jit(solution)/shard_map/all_gather | solution.py:138
  238.4 103.4 %copy-start.3 = (bf16[128,2048]{1,0:T(8,128)(2,1)}, bf16[128,2048]{1,0:T(8,128)(2,1)S(1)}, u32[]{:S(2)}) copy-start(bf16[128,2048]{1,0:T(8,128)(2,1)S(1)} %fusion.26) | copy-start | bytes 1572868
Sparse Core Ops, SparseCore 0:
  11.5 33.2 all-gather.8
  47.7 72.7 all-gather.6
  122.9 46.2 reduce-scatter.1
  170.8 30.5 all-gather.10
  203.0 30.8 all-gather.12
  239.5 93.0 all-gather.14
